TPU v7x, 512 devices: a whole 4x8x8 slice. The times are simulated.
512 devices in a mesh: gx: 64 (over z, x, core), gy: 8 (over y).
Axes of the slice: x: 4, y: 8, z: 8, core: 2. Of those that a mesh axis runs over, the one named last changes fastest.
Arguments:
- velocity: float32 [3, 128, 1536, 128], P(None, 'gx', 'gy'), may hold values from -0.8 to 2.3
- stiffness: float32 [8], P('gy'), may hold values from 100 to 100000
- block_inverse: float32 [3, 1536, 192], P(None, 'gy'), as said below
Outputs:
- velocity_next: float32 [3, 128, 1536, 128], P(None, 'gx', 'gy')
Inputs may be any that keep to these rules, and one draw needn't show every extreme that they name: block_inverse[s] for block k is, to float32 rounding, the inverse of the 192-row matrix with 1 + 2 b on its diagonal and -b beside it, b = alpha_s stiffness[k].
All inputs are finite; a program needn't handle non-finite values.
Results may differ from a plain program's by a relative error of at most 0.0003.
Values sent between devices are 32-bit elements; how exact they have to be, the bound alone decides.
No kernel may reach another device: no remote copies, remote signals or barrier semaphores. Data moves between devices by JAX's collectives and lax.ppermute only.
A program may use at most 64 MiB of HBM per device.

v0:
```python
import jax
import jax.numpy as jnp
from jax import lax
from jax.sharding import PartitionSpec as P

SUBSTEPS = 3
implicit_share = (8.0 / 15.0, 2.0 / 15.0, 1.0 / 3.0)
new_weight = (8.0 / 15.0, 5.0 / 12.0, 3.0 / 4.0)
old_weight = (0.0, -17.0 / 60.0, -5.0 / 12.0)
courant = (0.3, 0.2, 0.3)


def with_halo(cells, sides, width, closed):
    for axis, dim in sides:
        count = lax.axis_size(axis)
        ends = count if closed else count - 1
        head = lax.slice_in_dim(cells, 0, width, axis=dim)
        tail = lax.slice_in_dim(cells, cells.shape[dim] - width, cells.shape[dim], axis=dim)
        cells = jnp.concatenate(
            [
                lax.ppermute(tail, axis, [(i, (i + 1) % count) for i in range(ends)]),
                cells,
                lax.ppermute(head, axis, [((i + 1) % count, i) for i in range(ends)]),
            ],
            axis=dim,
        )
    return cells


def upwind(field, back_two, back_one, ahead_one, ahead_two, speed):
    behind = 1.5 * field - 2.0 * back_one + 0.5 * back_two
    ahead = -1.5 * field + 2.0 * ahead_one - 0.5 * ahead_two
    return jnp.maximum(speed, 0.0) * behind + jnp.minimum(speed, 0.0) * ahead


def reduced(first_vals, last_vals, tips):
    count = first_vals.shape[0]
    prev_q = jnp.zeros((), jnp.float32)
    prev_last = jnp.zeros_like(first_vals[0])
    fronts, backs, front_qs, back_qs = ([], [], [], [])
    for block in range(count):
        head_v = tips[0][block]
        tail_v = tips[1][block]
        head_w = tips[2][block]
        tail_w = tips[3][block]
        pivot = 1.0 - head_v * prev_q
        front = (first_vals[block] - head_v * prev_last) / pivot
        back = last_vals[block] - tail_v * prev_last + tail_v * prev_q * front
        front_q = head_w / pivot
        back_q = tail_w + tail_v * prev_q * front_q
        fronts.append(front)
        backs.append(back)
        front_qs.append(front_q)
        back_qs.append(back_q)
        prev_q = back_q
        prev_last = back
    heads = [None] * count
    tails = [None] * count
    heads[count - 1] = fronts[count - 1]
    tails[count - 1] = backs[count - 1]
    for block in range(count - 2, -1, -1):
        after = heads[block + 1]
        heads[block] = fronts[block] - front_qs[block] * after
        tails[block] = backs[block] - back_qs[block] * after
    zero = jnp.zeros_like(first_vals[0])
    lower_prev = jnp.stack([zero] + tails[:-1])
    upper_next = jnp.stack(heads[1:] + [zero])
    return (lower_prev, upper_next)


def body(velocity, stiffness, block_inverse):
    blocks = lax.axis_size("gy")
    own_index = lax.axis_index("gy")
    spans = velocity.shape[3]
    stiff = stiffness[0]
    first_flag = (own_index > 0).astype(jnp.float32)
    last_flag = (own_index < blocks - 1).astype(jnp.float32)
    coupling = -jnp.array(implicit_share, jnp.float32) * stiff
    lower = coupling * first_flag
    upper = coupling * last_flag
    column_v = block_inverse[:, :, 0] * lower[:, None]
    column_w = block_inverse[:, :, -1] * upper[:, None]
    own_tips = jnp.stack(
        [column_v[:, 0], column_v[:, -1], column_w[:, 0], column_w[:, -1]], axis=1
    )[:, :, None]
    every_tip = lax.all_gather(own_tips, "gy", axis=2, tiled=True)
    current = velocity
    previous = velocity
    for step in range(SUBSTEPS):
        widened = with_halo(current, (("gx", 1),), 2, True)
        middle = widened[:, 2:-2]
        ypadded = with_halo(middle, (("gy", 2),), 2, False)
        along_x = upwind(
            middle,
            widened[:, 0:-4],
            widened[:, 1:-3],
            widened[:, 3:-1],
            widened[:, 4:],
            middle[0:1],
        )
        along_y = upwind(
            middle,
            ypadded[:, :, 0:-4],
            ypadded[:, :, 1:-3],
            ypadded[:, :, 3:-1],
            ypadded[:, :, 4:],
            middle[1:2],
        )
        along_z = upwind(
            middle,
            jnp.roll(middle, 2, 3),
            jnp.roll(middle, 1, 3),
            jnp.roll(middle, -1, 3),
            jnp.roll(middle, -2, 3),
            middle[2:3],
        )
        advect = courant[0] * along_x + courant[1] * along_y + courant[2] * along_z
        diffuse = stiff * (ypadded[:, :, 3:-1] - 2.0 * middle + ypadded[:, :, 1:-3])
        forcing = middle + implicit_share[step] * diffuse - new_weight[step] * advect
        if step > 0:
            forcing = forcing - old_weight[step] * previous
        previous = advect
        planes = middle.shape[1]
        solved = jnp.einsum(
            "ij,cxjz->cxiz", block_inverse[step], forcing, precision=lax.Precision.HIGHEST
        )
        edges = jnp.stack([solved[:, :, 0, :], solved[:, :, -1, :]]).reshape(2, -1)
        tips = every_tip[step]
        grouped = lax.all_to_all(
            edges.reshape(2, blocks, -1), "gy", split_axis=1, concat_axis=1, tiled=True
        )
        lower_prev, upper_next = reduced(grouped[0], grouped[1], tips)
        returned = lax.all_to_all(
            jnp.stack([lower_prev, upper_next]), "gy", split_axis=1, concat_axis=1, tiled=True
        ).reshape(2, -1)
        lower_own = returned[0]
        upper_own = returned[1]
        lower_own = lower_own.reshape(3, planes, spans)[:, :, None, :]
        upper_own = upper_own.reshape(3, planes, spans)[:, :, None, :]
        current = (
            solved
            - column_v[step][None, None, :, None] * lower_own
            - column_w[step][None, None, :, None] * upper_own
        )
    return current


def solution(mesh):
    return jax.shard_map(
        body,
        mesh=mesh,
        in_specs=(P(None, "gx", "gy", None), P("gy"), P(None, "gy", None)),
        out_specs=P(None, "gx", "gy", None),
        check_vma=False,
    )
```

profile of v0, /device:TPU:8, one launch (start us, length us, event | category | flops | bytes accessed | tf_op | source)
XLA Modules:
  0.0 241.1 jit_solution(6409454955614664541)
XLA Ops:
  0.0 12.6 %collective-permute-start.3 = (f32[3,2,192,128]{3,2,1,0:T(8,128)}, f32[3,2,192,128]{3,2,1,0:T(8,128)}, u32[]{:S(2)}, u32[]{:S(2)}) collective-permute-start(f32[3,2,192,128]{3,2,1,0:T(8,128)} %param.4), channel_id=1, source_target_pairs={{8,0},{16,8},{24,16},{32,24},{40,32},{48,40},{56,48},{64,56},{72,6... | collective-permute-start | bytes 1769480 | tf_op jit(solution)/shard_map/ppermute | solution.py:23
  17.6 3.6 %collective-permute-start.1 = (f32[3,2,2,128]{3,2,1,0:T(2,128)S(1)}, f32[3,2,2,128]{3,2,1,0:T(2,128)S(1)}, u32[]{:S(2)}, u32[]{:S(2)}) collective-permute-start(f32[3,2,2,128]{3,2,1,0:T(2,128)S(1)} %get-tuple-element.146), channel_id=1, source_target_pairs={{0,1},{1,2},{2,3},{3,4},{4,5},{5,6},{6,7},{8,9},{9,10},{10,11},{11... | collective-permute-start | bytes 18440 | tf_op jit(solution)/shard_map/ppermute | solution.py:21
  28.6 23.4 %all_gather.3 = f32[3,4,8]{1,0,2:T(4,128)S(1)} all-gather(f32[3,4,1]{1,0,2:T(4,128)S(1)} %maximum_bitcast_fusion.9), channel_id=1, replica_groups=mesh['gx'=64,'gy'=8] {'gy'}, dimensions={2}, use_global_device_ids=true | all-gather | bytes 432 | tf_op jit(solution)/shard_map/all_gather | solution.py:86
  54.3 2.7 %fusion.61 = f32[3,2,192,128]{3,2,1,0:T(8,128)S(1)} fusion(f32[3,2,194,128]{3,2,1,0:T(8,128)S(1)} %constant_dynamic-update-slice_fusion, f32[3,2,192,128]{3,2,1,0:T(8,128)S(1)} %copy-done, f32[3,2,2,128]{3,2,1,0:T(2,128)S(1)} %copy-done.12, f32[3,2,192,128]{3,2,1,0:T(8,128)} %collective-permute-done.3, f32[3,2,192,128]{3,2,1,0:T(8,128)} %collective-permute-done.2, ...), kind=kLoop, calls=%fused_computation.79 | loop fusion | flops 7077888 | bytes 7084032 | tf_op jit(solution)/shard_map/add | solution.py:117
  59.7 5.2 %all-to-all-start = ((f32[2,8,96]{2,0,1:T(2,128)}), f32[2,8,96]{2,0,1:T(2,128)S(1)}, u32[]{:S(2)}, u32[]{:S(2)}) async-start(f32[2,8,96]{2,0,1:T(2,128)} %pad_maximum_fusion.11), calls=%async_computation | async-start | bytes 16384 | tf_op jit(solution)/shard_map/all_to_all | solution.py:129
  83.8 7.7 %fusion.235 = (f32[1,96]{1,0:T(1,128)S(1)}, f32[1,96]{1,0:T(1,128)S(1)}, f32[1,96]{1,0:T(1,128)S(1)}, f32[1,96]{1,0:T(1,128)S(1)}, f32[1,96]{1,0:T(1,128)S(1)}, ...) fusion(f32[2,8,96]{2,0,1:T(2,128)S(1)} %all-to-all-done, ...), kind=kLoop, calls=%fused_computation.345 | loop fusion | flops 4512 | bytes 10476 | tf_op jit(solution)/shard_map/add | solution.py:48
  92.9 7.2 %all-to-all-start.1 = ((f32[2,8,96]{2,0,1:T(2,128)}), f32[2,8,96]{2,0,1:T(2,128)S(1)}, u32[]{:S(2)}, u32[]{:S(2)}) async-start(f32[2,8,96]{2,0,1:T(2,128)} %copy.10), calls=%async_computation.1 | async-start | bytes 16384 | tf_op jit(solution)/shard_map/all_to_all | solution.py:133
  100.8 5.6 %all-to-all-done.1 = f32[2,8,96]{2,0,1:T(2,128)S(1)} async-done(((f32[2,8,96]{2,0,1:T(2,128)}), f32[2,8,96]{2,0,1:T(2,128)S(1)}, u32[]{:S(2)}, u32[]{:S(2)}) %all-to-all-start.1) | async-done | bytes 6176 | tf_op jit(solution)/shard_map/all_to_all | solution.py:133
  109.4 2.4 collective-permute-start.6
  112.5 3.3 %collective-permute-start.4 = (f32[3,2,2,128]{3,2,1,0:T(2,128)S(1)}, f32[3,2,2,128]{3,2,1,0:T(2,128)S(1)}, u32[]{:S(2)}, u32[]{:S(2)}) collective-permute-start(f32[3,2,2,128]{3,2,1,0:T(2,128)S(1)} %get-tuple-element.129), channel_id=1, source_target_pairs={{1,0},{2,1},{3,2},{4,3},{5,4},{6,5},{7,6},{9,8},{10,9},{11,10},{12... | collective-permute-start | bytes 18440 | tf_op jit(solution)/shard_map/ppermute | solution.py:23
  115.8 2.5 %collective-permute-start.5 = (f32[3,2,2,128]{3,2,1,0:T(2,128)S(1)}, f32[3,2,2,128]{3,2,1,0:T(2,128)S(1)}, u32[]{:S(2)}, u32[]{:S(2)}) collective-permute-start(f32[3,2,2,128]{3,2,1,0:T(2,128)S(1)} %get-tuple-element.128), channel_id=1, source_target_pairs={{0,1},{1,2},{2,3},{3,4},{4,5},{5,6},{6,7},{8,9},{9,10},{10,11},{11... | collective-permute-start | bytes 18440 | tf_op jit(solution)/shard_map/ppermute | solution.py:21
  118.6 2.7 %collective-permute-done.5 = f32[3,2,2,128]{3,2,1,0:T(2,128)S(1)} collective-permute-done((f32[3,2,2,128]{3,2,1,0:T(2,128)S(1)}, f32[3,2,2,128]{3,2,1,0:T(2,128)S(1)}, u32[]{:S(2)}, u32[]{:S(2)}) %collective-permute-start.5) | collective-permute-done | bytes 6176 | tf_op jit(solution)/shard_map/ppermute | solution.py:21
  121.3 2.5 %collective-permute-done.6 = f32[3,2,192,128]{3,2,1,0:T(8,128)S(1)} collective-permute-done((f32[3,2,192,128]{3,2,1,0:T(8,128)S(1)}, f32[3,2,192,128]{3,2,1,0:T(8,128)S(1)}, u32[]{:S(2)}, u32[]{:S(2)}) %collective-permute-start.6) | collective-permute-done | bytes 589856 | tf_op jit(solution)/shard_map/ppermute | solution.py:21
  127.0 4.7 %all-to-all-start.2 = ((f32[2,8,96]{2,0,1:T(2,128)}), f32[2,8,96]{2,0,1:T(2,128)S(1)}, u32[]{:S(2)}, u32[]{:S(2)}) async-start(f32[2,8,96]{2,0,1:T(2,128)} %pad_maximum_fusion.13), calls=%async_computation.2 | async-start | bytes 16384 | tf_op jit(solution)/shard_map/all_to_all | solution.py:129
  150.5 7.5 %fusion.206 = (f32[1,96]{1,0:T(1,128)S(1)}, f32[1,96]{1,0:T(1,128)S(1)}, f32[1,96]{1,0:T(1,128)S(1)}, f32[1,96]{1,0:T(1,128)S(1)}, f32[1,96]{1,0:T(1,128)S(1)}, ...) fusion(f32[2,8,96]{2,0,1:T(2,128)S(1)} %all-to-all-done.2, ...), kind=kLoop, calls=%fused_computation.301 | loop fusion | flops 4512 | bytes 10476 | tf_op jit(solution)/shard_map/add | solution.py:48
  158.8 13.3 %all_to_all.30 = f32[2,8,96]{2,0,1:T(2,128)S(1)} all-to-all(f32[2,8,96]{2,0,1:T(2,128)S(1)} %copy.13), channel_id=1, replica_groups=mesh['gx'=64,'gy'=8] {'gy'}, dimensions={1} | all-to-all | bytes 12288 | tf_op jit(solution)/shard_map/all_to_all | solution.py:133
  175.1 2.4 collective-permute-start.10
  178.2 3.3 %collective-permute-start.8 = (f32[3,2,2,128]{3,2,1,0:T(2,128)S(1)}, f32[3,2,2,128]{3,2,1,0:T(2,128)S(1)}, u32[]{:S(2)}, u32[]{:S(2)}) collective-permute-start(f32[3,2,2,128]{3,2,1,0:T(2,128)S(1)} %get-tuple-element.113), channel_id=1, source_target_pairs={{1,0},{2,1},{3,2},{4,3},{5,4},{6,5},{7,6},{9,8},{10,9},{11,10},{12... | collective-permute-start | bytes 18440 | tf_op jit(solution)/shard_map/ppermute | solution.py:23
  181.5 2.7 %collective-permute-start.9 = (f32[3,2,2,128]{3,2,1,0:T(2,128)S(1)}, f32[3,2,2,128]{3,2,1,0:T(2,128)S(1)}, u32[]{:S(2)}, u32[]{:S(2)}) collective-permute-start(f32[3,2,2,128]{3,2,1,0:T(2,128)S(1)} %get-tuple-element.112), channel_id=1, source_target_pairs={{0,1},{1,2},{2,3},{3,4},{4,5},{5,6},{6,7},{8,9},{9,10},{10,11},{11... | collective-permute-start | bytes 18440 | tf_op jit(solution)/shard_map/ppermute | solution.py:21
  184.6 2.5 %collective-permute-done.9 = f32[3,2,2,128]{3,2,1,0:T(2,128)S(1)} collective-permute-done((f32[3,2,2,128]{3,2,1,0:T(2,128)S(1)}, f32[3,2,2,128]{3,2,1,0:T(2,128)S(1)}, u32[]{:S(2)}, u32[]{:S(2)}) %collective-permute-start.9) | collective-permute-done | bytes 6176 | tf_op jit(solution)/shard_map/ppermute | solution.py:21
  187.1 2.5 %collective-permute-done.10 = f32[3,2,192,128]{3,2,1,0:T(8,128)S(1)} collective-permute-done((f32[3,2,192,128]{3,2,1,0:T(8,128)S(1)}, f32[3,2,192,128]{3,2,1,0:T(8,128)S(1)}, u32[]{:S(2)}, u32[]{:S(2)}) %collective-permute-start.10) | collective-permute-done | bytes 589856 | tf_op jit(solution)/shard_map/ppermute | solution.py:21
  192.7 4.7 %all-to-all-start.4 = ((f32[2,8,96]{2,0,1:T(2,128)}), f32[2,8,96]{2,0,1:T(2,128)S(1)}, u32[]{:S(2)}, u32[]{:S(2)}) async-start(f32[2,8,96]{2,0,1:T(2,128)} %pad_maximum_fusion.15), calls=%async_computation.4 | async-start | bytes 16384 | tf_op jit(solution)/shard_map/all_to_all | solution.py:129
  216.3 7.6 %fusion.177 = (f32[1,96]{1,0:T(1,128)S(1)}, f32[1,96]{1,0:T(1,128)S(1)}, f32[1,96]{1,0:T(1,128)S(1)}, f32[1,96]{1,0:T(1,128)S(1)}, f32[1,96]{1,0:T(1,128)S(1)}, ...) fusion(f32[2,8,96]{2,0,1:T(2,128)S(1)} %all-to-all-done.4, ...), kind=kLoop, calls=%fused_computation.257 | loop fusion | flops 4512 | bytes 10476 | tf_op jit(solution)/shard_map/add | solution.py:48
  225.3 13.3 %all_to_all.31 = f32[2,8,96]{2,0,1:T(2,128)S(1)} all-to-all(f32[2,8,96]{2,0,1:T(2,128)S(1)} %copy.16), channel_id=1, replica_groups=mesh['gx'=64,'gy'=8] {'gy'}, dimensions={1} | all-to-all | bytes 12288 | tf_op jit(solution)/shard_map/all_to_all | solution.py:133
  (153 shorter events, 39.4 us)
Async XLA Ops:
  0.0 53.1 %collective-permute-start.3 = (f32[3,2,192,128]{3,2,1,0:T(8,128)}, f32[3,2,192,128]{3,2,1,0:T(8,128)}, u32[]{:S(2)}, u32[]{:S(2)}) collective-permute-start(f32[3,2,192,128]{3,2,1,0:T(8,128)} %param.4), channel_id=1, source_target_pairs={{8,0},{16,8},{24,16},{32,24},{40,32},{48,40},{56,48},{64,56},{72,6... | collective-permute-start | bytes 1769480 | tf_op jit(solution)/shard_map/ppermute | solution.py:23
  12.6 40.5 %collective-permute-start.2 = (f32[3,2,192,128]{3,2,1,0:T(8,128)}, f32[3,2,192,128]{3,2,1,0:T(8,128)}, u32[]{:S(2)}, u32[]{:S(2)}) collective-permute-start(f32[3,2,192,128]{3,2,1,0:T(8,128)} %param.4), channel_id=1, source_target_pairs={{0,8},{8,16},{16,24},{24,32},{32,40},{40,48},{48,56},{56,64},{64,7... | collective-permute-start | bytes 1769480 | tf_op jit(solution)/shard_map/ppermute | solution.py:21
  15.3 37.7 %collective-permute-start = (f32[3,2,2,128]{3,2,1,0:T(2,128)S(1)}, f32[3,2,2,128]{3,2,1,0:T(2,128)S(1)}, u32[]{:S(2)}, u32[]{:S(2)}) collective-permute-start(f32[3,2,2,128]{3,2,1,0:T(2,128)S(1)} %get-tuple-element.147), channel_id=1, source_target_pairs={{1,0},{2,1},{3,2},{4,3},{5,4},{6,5},{7,6},{9,8},{10,9},{11,10},{12... | collective-permute-start | bytes 18440 | tf_op jit(solution)/shard_map/ppermute | solution.py:23
  17.6 5.2 %copy-start = (f32[3,2,192,128]{3,2,1,0:T(8,128)S(1)}, f32[3,2,192,128]{3,2,1,0:T(8,128)}, u32[]{:S(2)}) copy-start(f32[3,2,192,128]{3,2,1,0:T(8,128)} %param.4) | copy-start | bytes 1769476
  17.6 35.4 %collective-permute-start.1 = (f32[3,2,2,128]{3,2,1,0:T(2,128)S(1)}, f32[3,2,2,128]{3,2,1,0:T(2,128)S(1)}, u32[]{:S(2)}, u32[]{:S(2)}) collective-permute-start(f32[3,2,2,128]{3,2,1,0:T(2,128)S(1)} %get-tuple-element.146), channel_id=1, source_target_pairs={{0,1},{1,2},{2,3},{3,4},{4,5},{5,6},{6,7},{8,9},{9,10},{10,11},{11... | collective-permute-start | bytes 18440 | tf_op jit(solution)/shard_map/ppermute | solution.py:21
  24.2 1.7 copy-start.3
  52.0 1.7 copy-start.1
  52.0 1.6 copy-start.2
  52.0 1.6 copy-start.5
  59.7 24.0 %all-to-all-start = ((f32[2,8,96]{2,0,1:T(2,128)}), f32[2,8,96]{2,0,1:T(2,128)S(1)}, u32[]{:S(2)}, u32[]{:S(2)}) async-start(f32[2,8,96]{2,0,1:T(2,128)} %pad_maximum_fusion.11), calls=%async_computation | async-start | bytes 16384 | tf_op jit(solution)/shard_map/all_to_all | solution.py:129
  92.2 14.4 %copy-start.19 = (f32[1,192]{1,0:T(1,128)S(1)}, f32[1,192]{1,0:T(1,128)}, u32[]{:S(2)}) copy-start(f32[1,192]{1,0:T(1,128)} %get-tuple-element.237) | copy-start | bytes 2308
  92.2 66.5 %copy-start.13 = (f32[1,96]{1,0:T(1,128)}, f32[1,96]{1,0:T(1,128)S(1)}, u32[]{:S(2)}) copy-start(f32[1,96]{1,0:T(1,128)S(1)} %broadcast.6105) | copy-start | bytes 1156
  92.9 13.5 %all-to-all-start.1 = ((f32[2,8,96]{2,0,1:T(2,128)}), f32[2,8,96]{2,0,1:T(2,128)S(1)}, u32[]{:S(2)}, u32[]{:S(2)}) async-start(f32[2,8,96]{2,0,1:T(2,128)} %copy.10), calls=%async_computation.1 | async-start | bytes 16384 | tf_op jit(solution)/shard_map/all_to_all | solution.py:133
  107.4 13.9 %collective-permute-start.7 = (f32[3,2,192,128]{3,2,1,0:T(8,128)S(1)}, f32[3,2,192,128]{3,2,1,0:T(8,128)S(1)}, u32[]{:S(2)}, u32[]{:S(2)}) collective-permute-start(f32[3,2,192,128]{3,2,1,0:T(8,128)S(1)} %multiply_subtract_fusion.6), channel_id=1, source_target_pairs={{8,0},{16,8},{24,16},{32,24},{40,32},{48,40},{56,48},{64,56},{72,6... | collective-permute-start | bytes 1769480 | tf_op jit(solution)/shard_map/ppermute | solution.py:23
  109.4 14.5 %collective-permute-start.6 = (f32[3,2,192,128]{3,2,1,0:T(8,128)S(1)}, f32[3,2,192,128]{3,2,1,0:T(8,128)S(1)}, u32[]{:S(2)}, u32[]{:S(2)}) collective-permute-start(f32[3,2,192,128]{3,2,1,0:T(8,128)S(1)} %multiply_subtract_fusion.6), channel_id=1, source_target_pairs={{0,8},{8,16},{16,24},{24,32},{32,40},{40,48},{48,56},{56,64},{64,7... | collective-permute-start | bytes 1769480 | tf_op jit(solution)/shard_map/ppermute | solution.py:21
  112.5 6.2 %collective-permute-start.4 = (f32[3,2,2,128]{3,2,1,0:T(2,128)S(1)}, f32[3,2,2,128]{3,2,1,0:T(2,128)S(1)}, u32[]{:S(2)}, u32[]{:S(2)}) collective-permute-start(f32[3,2,2,128]{3,2,1,0:T(2,128)S(1)} %get-tuple-element.129), channel_id=1, source_target_pairs={{1,0},{2,1},{3,2},{4,3},{5,4},{6,5},{7,6},{9,8},{10,9},{11,10},{12... | collective-permute-start | bytes 18440 | tf_op jit(solution)/shard_map/ppermute | solution.py:23
  115.8 5.5 %collective-permute-start.5 = (f32[3,2,2,128]{3,2,1,0:T(2,128)S(1)}, f32[3,2,2,128]{3,2,1,0:T(2,128)S(1)}, u32[]{:S(2)}, u32[]{:S(2)}) collective-permute-start(f32[3,2,2,128]{3,2,1,0:T(2,128)S(1)} %get-tuple-element.128), channel_id=1, source_target_pairs={{0,1},{1,2},{2,3},{3,4},{4,5},{5,6},{6,7},{8,9},{9,10},{10,11},{11... | collective-permute-start | bytes 18440 | tf_op jit(solution)/shard_map/ppermute | solution.py:21
  127.0 23.5 %all-to-all-start.2 = ((f32[2,8,96]{2,0,1:T(2,128)}), f32[2,8,96]{2,0,1:T(2,128)S(1)}, u32[]{:S(2)}, u32[]{:S(2)}) async-start(f32[2,8,96]{2,0,1:T(2,128)} %pad_maximum_fusion.13), calls=%async_computation.2 | async-start | bytes 16384 | tf_op jit(solution)/shard_map/all_to_all | solution.py:129
  133.7 38.6 %copy-start.17 = (f32[1,192]{1,0:T(1,128)S(1)}, f32[1,192]{1,0:T(1,128)}, u32[]{:S(2)}) copy-start(f32[1,192]{1,0:T(1,128)} %get-tuple-element.236) | copy-start | bytes 2308
  173.2 13.9 %collective-permute-start.11 = (f32[3,2,192,128]{3,2,1,0:T(8,128)S(1)}, f32[3,2,192,128]{3,2,1,0:T(8,128)S(1)}, u32[]{:S(2)}, u32[]{:S(2)}) collective-permute-start(f32[3,2,192,128]{3,2,1,0:T(8,128)S(1)} %multiply_subtract_fusion.5), channel_id=1, source_target_pairs={{8,0},{16,8},{24,16},{32,24},{40,32},{48,40},{56,48},{64,56},{72,6... | collective-permute-start | bytes 1769480 | tf_op jit(solution)/shard_map/ppermute | solution.py:23
  175.1 14.5 %collective-permute-start.10 = (f32[3,2,192,128]{3,2,1,0:T(8,128)S(1)}, f32[3,2,192,128]{3,2,1,0:T(8,128)S(1)}, u32[]{:S(2)}, u32[]{:S(2)}) collective-permute-start(f32[3,2,192,128]{3,2,1,0:T(8,128)S(1)} %multiply_subtract_fusion.5), channel_id=1, source_target_pairs={{0,8},{8,16},{16,24},{24,32},{32,40},{40,48},{48,56},{56,64},{64,7... | collective-permute-start | bytes 1769480 | tf_op jit(solution)/shard_map/ppermute | solution.py:21
  178.2 6.4 %collective-permute-start.8 = (f32[3,2,2,128]{3,2,1,0:T(2,128)S(1)}, f32[3,2,2,128]{3,2,1,0:T(2,128)S(1)}, u32[]{:S(2)}, u32[]{:S(2)}) collective-permute-start(f32[3,2,2,128]{3,2,1,0:T(2,128)S(1)} %get-tuple-element.113), channel_id=1, source_target_pairs={{1,0},{2,1},{3,2},{4,3},{5,4},{6,5},{7,6},{9,8},{10,9},{11,10},{12... | collective-permute-start | bytes 18440 | tf_op jit(solution)/shard_map/ppermute | solution.py:23
  181.5 5.5 %collective-permute-start.9 = (f32[3,2,2,128]{3,2,1,0:T(2,128)S(1)}, f32[3,2,2,128]{3,2,1,0:T(2,128)S(1)}, u32[]{:S(2)}, u32[]{:S(2)}) collective-permute-start(f32[3,2,2,128]{3,2,1,0:T(2,128)S(1)} %get-tuple-element.112), channel_id=1, source_target_pairs={{0,1},{1,2},{2,3},{3,4},{4,5},{5,6},{6,7},{8,9},{9,10},{10,11},{11... | collective-permute-start | bytes 18440 | tf_op jit(solution)/shard_map/ppermute | solution.py:21
  192.7 23.6 %all-to-all-start.4 = ((f32[2,8,96]{2,0,1:T(2,128)}), f32[2,8,96]{2,0,1:T(2,128)S(1)}, u32[]{:S(2)}, u32[]{:S(2)}) async-start(f32[2,8,96]{2,0,1:T(2,128)} %pad_maximum_fusion.15), calls=%async_computation.4 | async-start | bytes 16384 | tf_op jit(solution)/shard_map/all_to_all | solution.py:129
  (13 other events, 14.1 us)
where the time goes:
time: 243 us; the launch traced here: 241 us
  starting transfers between devices  62.7 us (26%)
  between operations  55.7 us (23%)
  blocking collectives  50 us (21%)
  other arithmetic  34.1 us (14%)
  local copies, waits for them, and re-layouts  17.6 us (7%)
  waiting for transfers between devices  15.9 us (7%)
  matrix products  5.06 us (2%)
    all_to_all x2, blocking collectives, body(): lax.all_to_all(jnp.stack([lower_prev, upper_next]), 'gy', split_axis=1, c...  26.6 us
    ppermute x6, starting transfers between devices, with_halo(): lax.ppermute(head, axis, [((i + 1) % count, i) for i in range(ends)])  25.5 us
    all_gather x1, blocking collectives, body(): every_tip = lax.all_gather(own_tips, 'gy', axis=2, tiled=True)  23.4 us
    add x3, other arithmetic, reduced(): back = last_vals[block] - tail_v * prev_last + tail_v * prev_q * front  22.8 us
    ppermute x6, starting transfers between devices, with_halo(): lax.ppermute(tail, axis, [(i, (i + 1) % count) for i in range(ends)])  15.5 us
    all_to_all x3, starting transfers between devices, body(): lax.all_to_all(edges.reshape(2, blocks, -1), 'gy', split_axis=1, concat_a...  14.6 us
    ppermute x6, waiting for transfers between devices, with_halo(): lax.ppermute(tail, axis, [(i, (i + 1) % count) for i in range(ends)])  10.3 us
    all_to_all x1, starting transfers between devices, body(): lax.all_to_all(jnp.stack([lower_prev, upper_next]), 'gy', split_axis=1, c...  7.21 us
  transfers between devices with their start and end apart: 16, of which 5 were waited for; matrix products, arithmetic and copies ran while one was open for 5% of the time, Pallas kernels for 0%

commit v1 on v0

--- a/solution.py
+++ b/solution.py
@@ -83,7 +83,15 @@
     own_tips = jnp.stack(
         [column_v[:, 0], column_v[:, -1], column_w[:, 0], column_w[:, -1]], axis=1
     )[:, :, None]
-    every_tip = lax.all_gather(own_tips, "gy", axis=2, tiled=True)
+    every_tip = jnp.concatenate(
+        lax.all_to_all(
+            jnp.stack([own_tips] * lax.axis_size("gy"), axis=0),
+            axis_name="gy",
+            concat_axis=0,
+            split_axis=0,
+        ),
+        axis=2,
+    )
     current = velocity
     previous = velocity
     for step in range(SUBSTEPS):

time: 243 us -> 228 us (0.938)
  blocking collectives: 50 us -> 26.6 us
  starting transfers between devices: 62.7 us -> 72.1 us
  local copies, waits for them, and re-layouts: 17.6 us -> 14.9 us
    all_gather x1 -> x0, blocking collectives: 23.4 us -> none  [body(): every_tip = lax.all_gather(own_tips, 'gy', axis=2, tiled=True)]
    all_to_all x0 -> x1, starting transfers between devices: none -> 7.55 us  [body(): lax.all_to_all(jnp.stack([own_tips] * lax.axis_size('gy'), axis=0), axis_...]
    unnamed x44 -> x8, local copies, waits for them, and re-layouts: 4.78 us -> 0.9 us
  transfers between devices with their start and end apart: 16 -> 17, of which waited for: 5 -> 6; matrix products, arithmetic and copies ran while one was open for 5% -> 6% of each run, Pallas kernels for 0% -> 0%
where the time goes in v1:
time: 228 us; the launch traced here: 226 us
  starting transfers between devices  72.1 us (32%)
  between operations  55.3 us (24%)
  other arithmetic  34.2 us (15%)
  blocking collectives  26.6 us (12%)
  waiting for transfers between devices  17.9 us (8%)
  local copies, waits for them, and re-layouts  14.9 us (7%)
  matrix products  5.06 us (2%)
    ppermute x6, starting transfers between devices, with_halo(): lax.ppermute(head, axis, [((i + 1) % count, i) for i in range(ends)])  27.4 us
    all_to_all x2, blocking collectives, body(): lax.all_to_all(jnp.stack([lower_prev, upper_next]), 'gy', split_axis=1, c...  26.6 us
    add x3, other arithmetic, reduced(): back = last_vals[block] - tail_v * prev_last + tail_v * prev_q * front  22.2 us
    all_to_all x3, starting transfers between devices, body(): lax.all_to_all(edges.reshape(2, blocks, -1), 'gy', split_axis=1, concat_a...  15 us
    ppermute x6, starting transfers between devices, with_halo(): lax.ppermute(tail, axis, [(i, (i + 1) % count) for i in range(ends)])  14.9 us
    ppermute x6, waiting for transfers between devices, with_halo(): lax.ppermute(tail, axis, [(i, (i + 1) % count) for i in range(ends)])  10.8 us
    all_to_all x1, starting transfers between devices, body(): lax.all_to_all(jnp.stack([own_tips] * lax.axis_size('gy'), axis=0), axis_...  7.55 us
    all_to_all x1, starting transfers between devices, body(): lax.all_to_all(jnp.stack([lower_prev, upper_next]), 'gy', split_axis=1, c...  7.21 us
  transfers between devices with their start and end apart: 17, of which 6 were waited for; matrix products, arithmetic and copies ran while one was open for 6% of the time, Pallas kernels for 0%

profile of v1, /device:TPU:8, one launch (start us, length us, event | category | flops | bytes accessed | tf_op | source)
XLA Modules:
  0.0 226.0 jit_solution(848122234377416777)
XLA Ops:
  0.0 12.6 %collective-permute-start.3 = (f32[3,2,192,128]{3,2,1,0:T(8,128)}, f32[3,2,192,128]{3,2,1,0:T(8,128)}, u32[]{:S(2)}, u32[]{:S(2)}) collective-permute-start(f32[3,2,192,128]{3,2,1,0:T(8,128)} %param.4), channel_id=1, source_target_pairs={{8,0},{16,8},{24,16},{32,24},{40,32},{48,40},{56,48},{64,56},{72,6... | collective-permute-start | bytes 1769480 | tf_op jit(solution)/shard_map/ppermute | solution.py:23
  17.6 3.5 %collective-permute-start.1 = (f32[3,2,2,128]{3,2,1,0:T(2,128)S(1)}, f32[3,2,2,128]{3,2,1,0:T(2,128)S(1)}, u32[]{:S(2)}, u32[]{:S(2)}) collective-permute-start(f32[3,2,2,128]{3,2,1,0:T(2,128)S(1)} %get-tuple-element.146), channel_id=1, source_target_pairs={{0,1},{1,2},{2,3},{3,4},{4,5},{5,6},{6,7},{8,9},{9,10},{10,11},{11... | collective-permute-start | bytes 18440 | tf_op jit(solution)/shard_map/ppermute | solution.py:21
  25.0 7.5 %all-to-all-start.1 = ((f32[8,3,4,1]{2,3,1,0:T(1,128)}), f32[8,3,4,1]{2,3,1,0:T(1,128)S(1)}, u32[]{:S(2)}, u32[]{:S(2)}) async-start(f32[8,3,4,1]{2,3,1,0:T(1,128)} %stack.56), calls=%async_computation.1 | async-start | bytes 24576 | tf_op jit(solution)/shard_map/all_to_all | solution.py:87
  39.6 4.0 %fusion.61 = f32[3,2,192,128]{3,2,1,0:T(8,128)S(1)} fusion(f32[3,2,194,128]{3,2,1,0:T(8,128)S(1)} %constant_dynamic-update-slice_fusion, f32[3,2,192,128]{3,2,1,0:T(8,128)S(1)} %copy-done, f32[3,2,2,128]{3,2,1,0:T(2,128)S(1)} %collective-permute-done.1, f32[3,2,192,128]{3,2,1,0:T(8,128)} %collective-permute-done.3, ...), kind=kLoop, calls=%fused_computation.79 | loop fusion | flops 7077888 | bytes 7084032 | tf_op jit(solution)/shard_map/add | solution.py:125
  46.3 5.7 %all-to-all-start = ((f32[2,8,96]{2,0,1:T(2,128)}), f32[2,8,96]{2,0,1:T(2,128)S(1)}, u32[]{:S(2)}, u32[]{:S(2)}) async-start(f32[2,8,96]{2,0,1:T(2,128)} %pad_maximum_fusion.11), calls=%async_computation | async-start | bytes 16384 | tf_op jit(solution)/shard_map/all_to_all | solution.py:137
  70.6 7.3 %fusion.235 = (f32[1,96]{1,0:T(1,128)S(1)}, f32[1,96]{1,0:T(1,128)S(1)}, f32[1,96]{1,0:T(1,128)S(1)}, f32[1,96]{1,0:T(1,128)S(1)}, f32[1,96]{1,0:T(1,128)S(1)}, ...) fusion(f32[2,8,96]{2,0,1:T(2,128)S(1)} %all-to-all-done, ...), kind=kLoop, calls=%fused_computation.345 | loop fusion | flops 4512 | bytes 10476 | tf_op jit(solution)/shard_map/add | solution.py:48
  79.4 7.2 %all-to-all-start.2 = ((f32[2,8,96]{2,0,1:T(2,128)}), f32[2,8,96]{2,0,1:T(2,128)S(1)}, u32[]{:S(2)}, u32[]{:S(2)}) async-start(f32[2,8,96]{2,0,1:T(2,128)} %copy.10), calls=%async_computation.2 | async-start | bytes 16384 | tf_op jit(solution)/shard_map/all_to_all | solution.py:141
  87.3 5.6 %all-to-all-done.2 = f32[2,8,96]{2,0,1:T(2,128)S(1)} async-done(((f32[2,8,96]{2,0,1:T(2,128)}), f32[2,8,96]{2,0,1:T(2,128)S(1)}, u32[]{:S(2)}, u32[]{:S(2)}) %all-to-all-start.2) | async-done | bytes 6176 | tf_op jit(solution)/shard_map/all_to_all | solution.py:141
  93.2 3.9 %collective-permute-start.7 = (f32[3,2,192,128]{3,2,1,0:T(8,128)S(1)}, f32[3,2,192,128]{3,2,1,0:T(8,128)S(1)}, u32[]{:S(2)}, u32[]{:S(2)}) collective-permute-start(f32[3,2,192,128]{3,2,1,0:T(8,128)S(1)} %multiply_subtract_fusion.6), channel_id=1, source_target_pairs={{8,0},{16,8},{24,16},{32,24},{40,32},{48,40},{56,48},{64,56},{72,6... | collective-permute-start | bytes 1769480 | tf_op jit(solution)/shard_map/ppermute | solution.py:23
  99.7 3.3 %collective-permute-start.4 = (f32[3,2,2,128]{3,2,1,0:T(2,128)S(1)}, f32[3,2,2,128]{3,2,1,0:T(2,128)S(1)}, u32[]{:S(2)}, u32[]{:S(2)}) collective-permute-start(f32[3,2,2,128]{3,2,1,0:T(2,128)S(1)} %get-tuple-element.129), channel_id=1, source_target_pairs={{1,0},{2,1},{3,2},{4,3},{5,4},{6,5},{7,6},{9,8},{10,9},{11,10},{12... | collective-permute-start | bytes 18440 | tf_op jit(solution)/shard_map/ppermute | solution.py:23
  103.1 2.5 %collective-permute-start.5 = (f32[3,2,2,128]{3,2,1,0:T(2,128)S(1)}, f32[3,2,2,128]{3,2,1,0:T(2,128)S(1)}, u32[]{:S(2)}, u32[]{:S(2)}) collective-permute-start(f32[3,2,2,128]{3,2,1,0:T(2,128)S(1)} %get-tuple-element.128), channel_id=1, source_target_pairs={{0,1},{1,2},{2,3},{3,4},{4,5},{5,6},{6,7},{8,9},{9,10},{10,11},{11... | collective-permute-start | bytes 18440 | tf_op jit(solution)/shard_map/ppermute | solution.py:21
  105.9 2.7 %collective-permute-done.5 = f32[3,2,2,128]{3,2,1,0:T(2,128)S(1)} collective-permute-done((f32[3,2,2,128]{3,2,1,0:T(2,128)S(1)}, f32[3,2,2,128]{3,2,1,0:T(2,128)S(1)}, u32[]{:S(2)}, u32[]{:S(2)}) %collective-permute-start.5) | collective-permute-done | bytes 6176 | tf_op jit(solution)/shard_map/ppermute | solution.py:21
  108.6 3.0 %collective-permute-done.6 = f32[3,2,192,128]{3,2,1,0:T(8,128)S(1)} collective-permute-done((f32[3,2,192,128]{3,2,1,0:T(8,128)S(1)}, f32[3,2,192,128]{3,2,1,0:T(8,128)S(1)}, u32[]{:S(2)}, u32[]{:S(2)}) %collective-permute-start.6) | collective-permute-done | bytes 589856 | tf_op jit(solution)/shard_map/ppermute | solution.py:21
  114.8 4.7 %all-to-all-start.3 = ((f32[2,8,96]{2,0,1:T(2,128)}), f32[2,8,96]{2,0,1:T(2,128)S(1)}, u32[]{:S(2)}, u32[]{:S(2)}) async-start(f32[2,8,96]{2,0,1:T(2,128)} %pad_maximum_fusion.13), calls=%async_computation.3 | async-start | bytes 16384 | tf_op jit(solution)/shard_map/all_to_all | solution.py:137
  138.3 7.5 %fusion.206 = (f32[1,96]{1,0:T(1,128)S(1)}, f32[1,96]{1,0:T(1,128)S(1)}, f32[1,96]{1,0:T(1,128)S(1)}, f32[1,96]{1,0:T(1,128)S(1)}, f32[1,96]{1,0:T(1,128)S(1)}, ...) fusion(f32[2,8,96]{2,0,1:T(2,128)S(1)} %all-to-all-done.3, ...), kind=kLoop, calls=%fused_computation.301 | loop fusion | flops 4512 | bytes 10476 | tf_op jit(solution)/shard_map/add | solution.py:48
  146.7 13.3 %all_to_all.35 = f32[2,8,96]{2,0,1:T(2,128)S(1)} all-to-all(f32[2,8,96]{2,0,1:T(2,128)S(1)} %copy.13), channel_id=1, replica_groups=mesh['gx'=64,'gy'=8] {'gy'}, dimensions={1} | all-to-all | bytes 12288 | tf_op jit(solution)/shard_map/all_to_all | solution.py:141
  162.3 2.4 %collective-permute-start.10 = (f32[3,2,192,128]{3,2,1,0:T(8,128)S(1)}, f32[3,2,192,128]{3,2,1,0:T(8,128)S(1)}, u32[]{:S(2)}, u32[]{:S(2)}) collective-permute-start(f32[3,2,192,128]{3,2,1,0:T(8,128)S(1)} %multiply_subtract_fusion.5), channel_id=1, source_target_pairs={{0,8},{8,16},{16,24},{24,32},{32,40},{40,48},{48,56},{56,64},{64,7... | collective-permute-start | bytes 1769480 | tf_op jit(solution)/shard_map/ppermute | solution.py:21
  165.4 3.3 %collective-permute-start.8 = (f32[3,2,2,128]{3,2,1,0:T(2,128)S(1)}, f32[3,2,2,128]{3,2,1,0:T(2,128)S(1)}, u32[]{:S(2)}, u32[]{:S(2)}) collective-permute-start(f32[3,2,2,128]{3,2,1,0:T(2,128)S(1)} %get-tuple-element.113), channel_id=1, source_target_pairs={{1,0},{2,1},{3,2},{4,3},{5,4},{6,5},{7,6},{9,8},{10,9},{11,10},{12... | collective-permute-start | bytes 18440 | tf_op jit(solution)/shard_map/ppermute | solution.py:23
  168.8 2.7 %collective-permute-start.9 = (f32[3,2,2,128]{3,2,1,0:T(2,128)S(1)}, f32[3,2,2,128]{3,2,1,0:T(2,128)S(1)}, u32[]{:S(2)}, u32[]{:S(2)}) collective-permute-start(f32[3,2,2,128]{3,2,1,0:T(2,128)S(1)} %get-tuple-element.112), channel_id=1, source_target_pairs={{0,1},{1,2},{2,3},{3,4},{4,5},{5,6},{6,7},{8,9},{9,10},{10,11},{11... | collective-permute-start | bytes 18440 | tf_op jit(solution)/shard_map/ppermute | solution.py:21
  171.8 2.5 %collective-permute-done.9 = f32[3,2,2,128]{3,2,1,0:T(2,128)S(1)} collective-permute-done((f32[3,2,2,128]{3,2,1,0:T(2,128)S(1)}, f32[3,2,2,128]{3,2,1,0:T(2,128)S(1)}, u32[]{:S(2)}, u32[]{:S(2)}) %collective-permute-start.9) | collective-permute-done | bytes 6176 | tf_op jit(solution)/shard_map/ppermute | solution.py:21
  174.3 2.5 %collective-permute-done.10 = f32[3,2,192,128]{3,2,1,0:T(8,128)S(1)} collective-permute-done((f32[3,2,192,128]{3,2,1,0:T(8,128)S(1)}, f32[3,2,192,128]{3,2,1,0:T(8,128)S(1)}, u32[]{:S(2)}, u32[]{:S(2)}) %collective-permute-start.10) | collective-permute-done | bytes 589856 | tf_op jit(solution)/shard_map/ppermute | solution.py:21
  179.9 4.7 %all-to-all-start.5 = ((f32[2,8,96]{2,0,1:T(2,128)}), f32[2,8,96]{2,0,1:T(2,128)S(1)}, u32[]{:S(2)}, u32[]{:S(2)}) async-start(f32[2,8,96]{2,0,1:T(2,128)} %pad_maximum_fusion.15), calls=%async_computation.5 | async-start | bytes 16384 | tf_op jit(solution)/shard_map/all_to_all | solution.py:137
  203.3 7.4 %fusion.177 = (f32[1,96]{1,0:T(1,128)S(1)}, f32[1,96]{1,0:T(1,128)S(1)}, f32[1,96]{1,0:T(1,128)S(1)}, f32[1,96]{1,0:T(1,128)S(1)}, f32[1,96]{1,0:T(1,128)S(1)}, ...) fusion(f32[2,8,96]{2,0,1:T(2,128)S(1)} %all-to-all-done.5, ...), kind=kLoop, calls=%fused_computation.257 | loop fusion | flops 4512 | bytes 10476 | tf_op jit(solution)/shard_map/add | solution.py:48
  211.5 13.3 %all_to_all.36 = f32[2,8,96]{2,0,1:T(2,128)S(1)} all-to-all(f32[2,8,96]{2,0,1:T(2,128)S(1)} %copy.16), channel_id=1, replica_groups=mesh['gx'=64,'gy'=8] {'gy'}, dimensions={1} | all-to-all | bytes 12288 | tf_op jit(solution)/shard_map/all_to_all | solution.py:141
  (119 shorter events, 37.7 us)
Async XLA Ops:
  0.0 39.6 %collective-permute-start.3 = (f32[3,2,192,128]{3,2,1,0:T(8,128)}, f32[3,2,192,128]{3,2,1,0:T(8,128)}, u32[]{:S(2)}, u32[]{:S(2)}) collective-permute-start(f32[3,2,192,128]{3,2,1,0:T(8,128)} %param.4), channel_id=1, source_target_pairs={{8,0},{16,8},{24,16},{32,24},{40,32},{48,40},{56,48},{64,56},{72,6... | collective-permute-start | bytes 1769480 | tf_op jit(solution)/shard_map/ppermute | solution.py:23
  12.6 27.0 %collective-permute-start.2 = (f32[3,2,192,128]{3,2,1,0:T(8,128)}, f32[3,2,192,128]{3,2,1,0:T(8,128)}, u32[]{:S(2)}, u32[]{:S(2)}) collective-permute-start(f32[3,2,192,128]{3,2,1,0:T(8,128)} %param.4), channel_id=1, source_target_pairs={{0,8},{8,16},{16,24},{24,32},{32,40},{40,48},{48,56},{56,64},{64,7... | collective-permute-start | bytes 1769480 | tf_op jit(solution)/shard_map/ppermute | solution.py:21
  15.3 24.3 %collective-permute-start = (f32[3,2,2,128]{3,2,1,0:T(2,128)S(1)}, f32[3,2,2,128]{3,2,1,0:T(2,128)S(1)}, u32[]{:S(2)}, u32[]{:S(2)}) collective-permute-start(f32[3,2,2,128]{3,2,1,0:T(2,128)S(1)} %get-tuple-element.147), channel_id=1, source_target_pairs={{1,0},{2,1},{3,2},{4,3},{5,4},{6,5},{7,6},{9,8},{10,9},{11,10},{12... | collective-permute-start | bytes 18440 | tf_op jit(solution)/shard_map/ppermute | solution.py:23
  17.6 22.0 %collective-permute-start.1 = (f32[3,2,2,128]{3,2,1,0:T(2,128)S(1)}, f32[3,2,2,128]{3,2,1,0:T(2,128)S(1)}, u32[]{:S(2)}, u32[]{:S(2)}) collective-permute-start(f32[3,2,2,128]{3,2,1,0:T(2,128)S(1)} %get-tuple-element.146), channel_id=1, source_target_pairs={{0,1},{1,2},{2,3},{3,4},{4,5},{5,6},{6,7},{8,9},{9,10},{10,11},{11... | collective-permute-start | bytes 18440 | tf_op jit(solution)/shard_map/ppermute | solution.py:21
  21.8 10.7 %copy-start = (f32[3,2,192,128]{3,2,1,0:T(8,128)S(1)}, f32[3,2,192,128]{3,2,1,0:T(8,128)}, u32[]{:S(2)}) copy-start(f32[3,2,192,128]{3,2,1,0:T(8,128)} %param.4) | copy-start | bytes 1769476
  23.4 0.7 copy-start.2
  25.0 13.9 %all-to-all-start.1 = ((f32[8,3,4,1]{2,3,1,0:T(1,128)}), f32[8,3,4,1]{2,3,1,0:T(1,128)S(1)}, u32[]{:S(2)}, u32[]{:S(2)}) async-start(f32[8,3,4,1]{2,3,1,0:T(1,128)} %stack.56), calls=%async_computation.1 | async-start | bytes 24576 | tf_op jit(solution)/shard_map/all_to_all | solution.py:87
  46.3 24.4 %all-to-all-start = ((f32[2,8,96]{2,0,1:T(2,128)}), f32[2,8,96]{2,0,1:T(2,128)S(1)}, u32[]{:S(2)}, u32[]{:S(2)}) async-start(f32[2,8,96]{2,0,1:T(2,128)} %pad_maximum_fusion.11), calls=%async_computation | async-start | bytes 16384 | tf_op jit(solution)/shard_map/all_to_all | solution.py:137
  79.4 13.5 %all-to-all-start.2 = ((f32[2,8,96]{2,0,1:T(2,128)}), f32[2,8,96]{2,0,1:T(2,128)S(1)}, u32[]{:S(2)}, u32[]{:S(2)}) async-start(f32[2,8,96]{2,0,1:T(2,128)} %copy.10), calls=%async_computation.2 | async-start | bytes 16384 | tf_op jit(solution)/shard_map/all_to_all | solution.py:141
  93.2 15.4 %collective-permute-start.7 = (f32[3,2,192,128]{3,2,1,0:T(8,128)S(1)}, f32[3,2,192,128]{3,2,1,0:T(8,128)S(1)}, u32[]{:S(2)}, u32[]{:S(2)}) collective-permute-start(f32[3,2,192,128]{3,2,1,0:T(8,128)S(1)} %multiply_subtract_fusion.6), channel_id=1, source_target_pairs={{8,0},{16,8},{24,16},{32,24},{40,32},{48,40},{56,48},{64,56},{72,6... | collective-permute-start | bytes 1769480 | tf_op jit(solution)/shard_map/ppermute | solution.py:23
  97.1 14.5 %collective-permute-start.6 = (f32[3,2,192,128]{3,2,1,0:T(8,128)S(1)}, f32[3,2,192,128]{3,2,1,0:T(8,128)S(1)}, u32[]{:S(2)}, u32[]{:S(2)}) collective-permute-start(f32[3,2,192,128]{3,2,1,0:T(8,128)S(1)} %multiply_subtract_fusion.6), channel_id=1, source_target_pairs={{0,8},{8,16},{16,24},{24,32},{32,40},{40,48},{48,56},{56,64},{64,7... | collective-permute-start | bytes 1769480 | tf_op jit(solution)/shard_map/ppermute | solution.py:21
  99.7 6.2 %collective-permute-start.4 = (f32[3,2,2,128]{3,2,1,0:T(2,128)S(1)}, f32[3,2,2,128]{3,2,1,0:T(2,128)S(1)}, u32[]{:S(2)}, u32[]{:S(2)}) collective-permute-start(f32[3,2,2,128]{3,2,1,0:T(2,128)S(1)} %get-tuple-element.129), channel_id=1, source_target_pairs={{1,0},{2,1},{3,2},{4,3},{5,4},{6,5},{7,6},{9,8},{10,9},{11,10},{12... | collective-permute-start | bytes 18440 | tf_op jit(solution)/shard_map/ppermute | solution.py:23
  103.1 5.5 %collective-permute-start.5 = (f32[3,2,2,128]{3,2,1,0:T(2,128)S(1)}, f32[3,2,2,128]{3,2,1,0:T(2,128)S(1)}, u32[]{:S(2)}, u32[]{:S(2)}) collective-permute-start(f32[3,2,2,128]{3,2,1,0:T(2,128)S(1)} %get-tuple-element.128), channel_id=1, source_target_pairs={{0,1},{1,2},{2,3},{3,4},{4,5},{5,6},{6,7},{8,9},{9,10},{10,11},{11... | collective-permute-start | bytes 18440 | tf_op jit(solution)/shard_map/ppermute | solution.py:21
  111.6 1.3 copy-start.1
  114.8 23.5 %all-to-all-start.3 = ((f32[2,8,96]{2,0,1:T(2,128)}), f32[2,8,96]{2,0,1:T(2,128)S(1)}, u32[]{:S(2)}, u32[]{:S(2)}) async-start(f32[2,8,96]{2,0,1:T(2,128)} %pad_maximum_fusion.13), calls=%async_computation.3 | async-start | bytes 16384 | tf_op jit(solution)/shard_map/all_to_all | solution.py:137
  160.4 13.9 %collective-permute-start.11 = (f32[3,2,192,128]{3,2,1,0:T(8,128)S(1)}, f32[3,2,192,128]{3,2,1,0:T(8,128)S(1)}, u32[]{:S(2)}, u32[]{:S(2)}) collective-permute-start(f32[3,2,192,128]{3,2,1,0:T(8,128)S(1)} %multiply_subtract_fusion.5), channel_id=1, source_target_pairs={{8,0},{16,8},{24,16},{32,24},{40,32},{48,40},{56,48},{64,56},{72,6... | collective-permute-start | bytes 1769480 | tf_op jit(solution)/shard_map/ppermute | solution.py:23
  162.3 14.5 %collective-permute-start.10 = (f32[3,2,192,128]{3,2,1,0:T(8,128)S(1)}, f32[3,2,192,128]{3,2,1,0:T(8,128)S(1)}, u32[]{:S(2)}, u32[]{:S(2)}) collective-permute-start(f32[3,2,192,128]{3,2,1,0:T(8,128)S(1)} %multiply_subtract_fusion.5), channel_id=1, source_target_pairs={{0,8},{8,16},{16,24},{24,32},{32,40},{40,48},{48,56},{56,64},{64,7... | collective-permute-start | bytes 1769480 | tf_op jit(solution)/shard_map/ppermute | solution.py:21
  165.4 6.4 %collective-permute-start.8 = (f32[3,2,2,128]{3,2,1,0:T(2,128)S(1)}, f32[3,2,2,128]{3,2,1,0:T(2,128)S(1)}, u32[]{:S(2)}, u32[]{:S(2)}) collective-permute-start(f32[3,2,2,128]{3,2,1,0:T(2,128)S(1)} %get-tuple-element.113), channel_id=1, source_target_pairs={{1,0},{2,1},{3,2},{4,3},{5,4},{6,5},{7,6},{9,8},{10,9},{11,10},{12... | collective-permute-start | bytes 18440 | tf_op jit(solution)/shard_map/ppermute | solution.py:23
  168.8 5.5 %collective-permute-start.9 = (f32[3,2,2,128]{3,2,1,0:T(2,128)S(1)}, f32[3,2,2,128]{3,2,1,0:T(2,128)S(1)}, u32[]{:S(2)}, u32[]{:S(2)}) collective-permute-start(f32[3,2,2,128]{3,2,1,0:T(2,128)S(1)} %get-tuple-element.112), channel_id=1, source_target_pairs={{0,1},{1,2},{2,3},{3,4},{4,5},{5,6},{6,7},{8,9},{9,10},{10,11},{11... | collective-permute-start | bytes 18440 | tf_op jit(solution)/shard_map/ppermute | solution.py:21
  179.9 23.4 %all-to-all-start.5 = ((f32[2,8,96]{2,0,1:T(2,128)}), f32[2,8,96]{2,0,1:T(2,128)S(1)}, u32[]{:S(2)}, u32[]{:S(2)}) async-start(f32[2,8,96]{2,0,1:T(2,128)} %pad_maximum_fusion.15), calls=%async_computation.5 | async-start | bytes 16384 | tf_op jit(solution)/shard_map/all_to_all | solution.py:137
